TPU v7x, 32 devices: a whole 2x2x4 slice. The times are simulated.
32 devices in a mesh: rep: 2 (over y), seq: 4 (over z), tp: 2 (over x), sub: 2 (over core).
Axes of the slice: x: 2, y: 2, z: 4, core: 2. Of those that a mesh axis runs over, the one named last changes fastest.
Arguments:
- latents: bfloat16 [3072, 3072], P(('rep', 'seq')), parts along dimension 0, may hold values from -6 to 6
- w_qkv: bfloat16 [3072, 3, 24, 128], P('seq', None, ('tp', 'sub')), may hold values from -0.109375 to 0.109375
- w_out: bfloat16 [24, 128, 3072], P(('tp', 'sub'), None, 'seq'), may hold values from -0.15625 to 0.15625
- query_gain: float32 [128], replicated, may hold values from 1.5 to 20
- key_gain: float32 [128], replicated, may hold values from 1.5 to 20
- mod_shift: float32 [6144], P('rep'), parts along dimension 0, may hold values from -3 to 3
- mod_scale: float32 [6144], P('rep'), parts along dimension 0, may hold values from -0.5 to 0.5
- mod_gate: float32 [6144], P('rep'), parts along dimension 0, may hold values from 0.5 to 1.5
- block_list: int32 [8, 9], P(('rep', 'seq')), parts along dimension 0, may hold values from 0 to 3, as said below
- block_live: int32 [8, 9], P(('rep', 'seq')), parts along dimension 0, may hold values from 0 to 1, as said below
- key_valid: int32 [3072], P(('rep', 'seq')), parts along dimension 0, may hold values from 0 to 1, as said below
Outputs:
- block_out: bfloat16 [3072, 3072], P(('rep', 'seq'), ('tp', 'sub')), parts along dimension 0
There are 2 independent parts, one for each index of `rep`. A program takes and returns all parts, laid end to end along the dimension named above; an argument that names none is the same for every part. Nothing has to cross between parts.
Inputs may be any that keep to these rules, and one draw needn't show every extreme that they name: `block_list`: tiles are numbered frame by frame, 2 tiles to a frame of tiles. Row a lists, in a drawn order, the tiles within 1 frames of tiles and 1 tile column of tile a; entries outside the video or dropped have block_live 0, and those outside the video repeat a. Live entries are distinct, and a itself is always live. `block_live`: see block_list. `key_valid`: within each tile either all tokens are real or the last 144 are padding.
All inputs are finite; a program needn't handle non-finite values.
Results may differ from a plain program's by a relative error of at most 0.012.
The roundings to bfloat16 on the way count: a program that leaves them out, or rounds other values in their place, can miss the bound.
Values may be sent and summed in bfloat16 or wider, within the bound.
No kernel may reach another device: no remote copies, remote signals or barrier semaphores. Data moves between devices by JAX's collectives and lax.ppermute only.
A program may use at most 128 MiB of HBM per device.

v0:
```python
import math
import jax
import jax.numpy as jnp
from jax import lax
from jax.sharding import PartitionSpec as P

HD = 128
TILE = 384


def modulate(latents, mod_shift, mod_scale):
    x_float = latents.astype(jnp.float32)
    centre = x_float - jnp.mean(x_float, axis=-1, keepdims=True)
    spread = jnp.mean(centre * centre, axis=-1, keepdims=True)
    return (centre * lax.rsqrt(spread + 1e-06) * (1.0 + mod_scale) + mod_shift).astype(jnp.bfloat16)


def head_norm(raw_heads, gain):
    square = jnp.mean(raw_heads * raw_heads, axis=-1, keepdims=True)
    return (raw_heads * lax.rsqrt(square + 1e-06) * gain).astype(jnp.bfloat16)


def add_rows(normed, block_rows):
    return jnp.einsum("td,dshe->tshe", normed, block_rows, preferred_element_type=jnp.float32)


def attend_piece(queries, tile_rows, state_now, pieces):
    key_rows, value_rows, key_ok = pieces
    row_count = key_rows.shape[0]
    tile_of = jnp.arange(row_count, dtype=jnp.int32) // TILE
    one_hot = (tile_of[None, :] == jnp.arange(tile_rows.shape[1], dtype=jnp.int32)[:, None]).astype(
        jnp.bfloat16
    )
    allowed = (jnp.dot(tile_rows, one_hot, preferred_element_type=jnp.float32) > 0.5) & (
        key_ok[None, :] > 0
    )
    score_scale = 1.0 / math.sqrt(HD)
    old_peak, old_total, weighted = state_now
    scores = (
        jnp.einsum("qhe,khe->hqk", queries, key_rows, preferred_element_type=jnp.float32)
        * score_scale
    )
    masked = jnp.where(allowed[None], scores, -1e30)
    new_peak = jnp.maximum(old_peak, jnp.max(masked, axis=2))
    weights = jnp.where(allowed[None], jnp.exp(masked - new_peak[:, :, None]), 0.0)
    new_total = jnp.sum(weights, axis=2)
    added = jnp.einsum(
        "hqk,khe->qhe", weights.astype(jnp.bfloat16), value_rows, preferred_element_type=jnp.float32
    )
    return (new_peak, new_total, added)


def local(
    latents,
    w_qkv,
    w_out,
    query_gain,
    key_gain,
    mod_shift,
    mod_scale,
    mod_gate,
    block_list,
    block_live,
    key_valid,
):
    tok_rows = latents.shape[0]
    heads_here = w_qkv.shape[2]
    tiles_all = block_list.shape[0] * lax.axis_size("seq")
    normed = modulate(latents, mod_shift, mod_scale)
    qkv = add_rows(normed, lax.all_gather(w_qkv, "seq", axis=0, tiled=True))
    queries = head_norm(qkv[:, 0], query_gain)
    key_rows = head_norm(qkv[:, 1], key_gain)
    value_rows = qkv[:, 2].astype(jnp.bfloat16)
    tile_ids = jnp.arange(tiles_all, dtype=jnp.int32)
    tile_hits = jnp.any(
        (block_list[:, :, None] == tile_ids[None, None, :]) & (block_live[:, :, None] > 0), axis=1
    )
    tile_rows = jnp.repeat(tile_hits.astype(jnp.bfloat16), TILE, axis=0)
    start_state = (
        jnp.full((heads_here, tok_rows), -1e30, jnp.float32),
        jnp.zeros((heads_here, tok_rows), jnp.float32),
        jnp.zeros((tok_rows, heads_here, HD), jnp.float32),
    )
    final_peak, final_total, weighted = attend_piece(
        queries,
        tile_rows,
        start_state,
        (
            lax.all_gather(key_rows, "seq", axis=0, tiled=True),
            lax.all_gather(value_rows, "seq", axis=0, tiled=True),
            lax.all_gather(key_valid, "seq", axis=0, tiled=True),
        ),
    )
    attended = (weighted / jnp.transpose(final_total)[:, :, None]).astype(jnp.bfloat16)
    head_terms = jnp.einsum(
        "the,hec->tc",
        attended,
        lax.all_gather(w_out, "seq", axis=2, tiled=True),
        preferred_element_type=jnp.float32,
    )
    projected = lax.psum_scatter(
        head_terms.astype(jnp.bfloat16), ("tp", "sub"), scatter_dimension=1, tiled=True
    ).astype(jnp.float32)
    out_width = projected.shape[1]
    offset = lax.axis_index(("tp", "sub")) * out_width
    latent_cols = lax.dynamic_slice_in_dim(latents, offset, out_width, 1).astype(jnp.float32)
    gate_cols = lax.dynamic_slice_in_dim(mod_gate, offset, out_width, 0)
    return (latent_cols + gate_cols * projected).astype(jnp.bfloat16)


def solution(mesh):
    in_specs = (
        P(("rep", "seq"), None),
        P("seq", None, ("tp", "sub"), None),
        P(("tp", "sub"), None, "seq"),
        P(),
        P(),
        P("rep"),
        P("rep"),
        P("rep"),
        P(("rep", "seq"), None),
        P(("rep", "seq"), None),
        P(("rep", "seq")),
    )
    out_specs = P(("rep", "seq"), ("tp", "sub"))
    return jax.shard_map(local, mesh=mesh, in_specs=in_specs, out_specs=out_specs, check_vma=False)
```

profile of v0, /device:TPU:0, one launch (start us, length us, event | category | flops | bytes accessed | tf_op | source)
XLA Modules:
  0.0 515.9 jit_solution(16770260743124015059)
XLA Ops:
  6.5 6.0 %copy.22 = bf16[768,3,6,128]{0,3,2,1:T(8,128)(2,1)} copy(bf16[768,3,6,128]{3,0,2,1:T(8,128)(2,1)} %param.12) | data formatting | bytes 7077888 | tf_op args[1]
  12.7 1.6 copy-done.1
  14.3 0.4 convert_reduce_fusion
  14.6 0.8 fusion.8
  15.4 244.0 %all-gather.7.cloned.1.call-done = bf16[3072,3,6,128]{0,3,2,1:T(8,128)(2,1)} async-done(((bf16[768,3,6,128]{0,3,2,1:T(8,128)(2,1)}), bf16[3072,3,6,128]{0,3,2,1:T(8,128)(2,1)}) %all-gather.7.cloned.1.call-update) | async-done | bytes 14155792 | tf_op jit(solution)/shard_map/all_gather | solution.py:70
  259.4 10.7 %fusion.13 = f32[384,2304]{0,1:S(1)} fusion(bf16[3072,2304]{0,1:T(8,128)(2,1)} %bitcast.46, bf16[384,3072]{1,0:T(8,128)(2,1)S(1)} %copy-done.1, f32[3072]{0:T(1024)S(1)} %copy-done.7, f32[3072]{0:T(1024)S(1)} %broadcast_add_fusion, f32[384]{0:T(512)S(1)} %add_rsqrt_fusion.2, f32[384]{0:T(512)S(1)} %broadcast_multiply_fusion), kind=kOutput, calls=%fused_computation.18 | convolution fusion | flops 5442895872 | bytes 20081664
  270.1 0.2 multiply_reduce_fusion.1
  270.3 1.5 copy-done.2
  271.8 1.0 multiply_convert_fusion
  272.9 0.7 all-gather.11.cloned.1.call-update
  273.6 2.2 slice.28
  275.9 12.4 %all-gather.1 = s32[4,1,384]{2,1,0:T(1,128)S(1)} all-gather(s32[1,1,384]{2,1,0:T(1,128)S(1)} %reshape.138), channel_id=1, replica_groups=mesh['rep'=2,'seq'=4,'tp'=2,'sub'=2] {'seq'}, dimensions={0}, use_global_device_ids=true | all-gather | bytes 7680 | tf_op jit(solution)/shard_map/all_gather | solution.py:91
  288.4 0.1 fusion.43
  288.5 0.5 fusion.12
  289.1 32.4 %all-gather.9.cloned.1.call-done = bf16[1536,6,128]{0,2,1:T(8,128)(2,1)} async-done(((bf16[384,6,128]{0,2,1:T(8,128)(2,1)}), bf16[1536,6,128]{0,2,1:T(8,128)(2,1)}) %all-gather.9.cloned.1.call-update) | async-done | bytes 2359312 | tf_op jit(solution)/shard_map/all_gather | solution.py:89
  321.5 5.0 fusion
  326.5 5.9 %copy-done = f32[6,384,1536]{2,1,0:T(8,128)} copy-done((f32[6,384,1536]{2,1,0:T(8,128)}, f32[6,384,1536]{2,1,0:T(8,128)S(1)}, u32[]{:S(2)}) %copy-start) | copy-done | bytes 14155800
  332.4 4.2 fusion.1
  336.6 74.5 %all-gather.11.cloned.1.call-done = bf16[6,128,3072]{2,1,0:T(8,128)(2,1)} async-done(((bf16[6,128,768]{2,1,0:T(8,128)(2,1)}), bf16[6,128,3072]{2,1,0:T(8,128)(2,1)}) %all-gather.11.cloned.1.call-update) | async-done | bytes 4718608 | tf_op jit(solution)/shard_map/all_gather | solution.py:98
  411.1 50.1 %all-gather.13.cloned.1.call-done = bf16[1536,1,6,128]{0,3,2,1:T(8,128)(2,1)} async-done(((bf16[384,1,6,128]{0,3,2,1:T(8,128)(2,1)}), bf16[1536,1,6,128]{0,3,2,1:T(8,128)(2,1)}) %all-gather.13.cloned.1.call-update) | async-done | bytes 2359312 | tf_op jit(solution)/shard_map/all_gather | solution.py:90
  461.2 14.5 %bitcast_convert_fusion = bf16[384,3072]{1,0:T(8,128)(2,1)} fusion(bf16[6,128,3072]{2,1,0:T(8,128)(2,1)} %all-gather.11.cloned.1.call-done, f32[6,384,1536]{2,1,0:T(8,128)} %copy-done, f32[6,384]{1,0:T(8,128)S(1)} %broadcast_maximum_fusion, pred[384,1536]{1,0:T(8,128)(4,1)S(1)} %fusion.12, bf16[1536,1,6,128]{0,3,2,1:T(8,128)(2,1)} %all-gather.13.cloned.1.call-done, ...), kind=kOutput, calls=%fused_computation.15 | convolution fusion | flops 2737373184 | bytes 24201216 | tf_op jit(solution)/shard_map/the,hec->tc/dot_general | solution.py:95
  475.7 0.8 dynamic_slice.7
  476.5 30.8 %reduce-scatter.2.cloned.1.call-done = bf16[384,768]{1,0:T(8,128)(2,1)} async-done(((bf16[384,3072]{1,0:T(8,128)(2,1)}), bf16[384,768]{1,0:T(8,128)(2,1)}) %reduce-scatter.2.cloned.1.call-update) | async-done | bytes 589840 | tf_op jit(solution)/shard_map/reduce_scatter | solution.py:101
  507.3 2.1 add_convert_fusion
  (38 shorter events, 0.4 us)
Async XLA Ops:
  6.5 252.9 %all-gather.7.cloned.1.call-start = ((), (), s32[]{:S(2)}) async-start(), calls=%async_computation.1 | async-start | bytes 17694720 | tf_op jit(solution)/shard_map/all_gather | solution.py:70
  12.6 1.7 copy-start.1
  12.6 2.8 copy-start.3
  12.6 246.8 %copy-start.7 = (f32[3072]{0:T(1024)S(1)}, f32[3072]{0:T(1024)}, u32[]{:S(2)}) copy-start(f32[3072]{0:T(1024)} %param.16) | copy-start | bytes 36868
  12.6 308.9 %all-gather.9.cloned.1.call-start = ((), (), s32[]{:S(2)}) async-start(), calls=%async_computation.2 | async-start | bytes 2949120 | tf_op jit(solution)/shard_map/all_gather | solution.py:89
  259.4 12.4 %copy-start.6 = (f32[128]{0:T(128)S(1)}, f32[128]{0:T(128)}, u32[]{:S(2)}) copy-start(f32[128]{0:T(128)} %param.15) | copy-start | bytes 1540
  270.1 1.8 copy-start.2
  270.1 5.8 %copy-start.4 = (s32[384]{0:T(512)S(1)}, s32[384]{0:T(512)}, u32[]{:S(2)}) copy-start(s32[384]{0:T(512)} %param.21) | copy-start | bytes 4612
  270.1 18.3 %copy-start.8 = (s32[1,9]{1,0:T(1,128)S(1)}, s32[1,9]{1,0:T(1,128)}, u32[]{:S(2)}) copy-start(s32[1,9]{1,0:T(1,128)} %param.20) | copy-start | bytes 112
  270.1 18.3 %copy-start.9 = (s32[1,9]{1,0:T(1,128)S(1)}, s32[1,9]{1,0:T(1,128)}, u32[]{:S(2)}) copy-start(s32[1,9]{1,0:T(1,128)} %param.19) | copy-start | bytes 112
  272.8 48.6 %copy-start.5 = (f32[128]{0:T(128)S(1)}, f32[128]{0:T(128)}, u32[]{:S(2)}) copy-start(f32[128]{0:T(128)} %param.14) | copy-start | bytes 1540
  272.9 138.2 %all-gather.11.cloned.1.call-start = ((), (), s32[]{:S(2)}) async-start(), calls=%async_computation.3 | async-start | bytes 5898240 | tf_op jit(solution)/shard_map/all_gather | solution.py:98
  273.6 187.6 %all-gather.13.cloned.1.call-start = ((), (), s32[]{:S(2)}) async-start(), calls=%async_computation.5 | async-start | bytes 2949120 | tf_op jit(solution)/shard_map/all_gather | solution.py:90
  275.8 231.5 %reduce-scatter.2.cloned.1.call-start = ((), (), s32[]{:S(2)}) async-start(), calls=%async_computation.4 | async-start | bytes 2949120 | tf_op jit(solution)/shard_map/reduce_scatter | solution.py:101
  326.5 5.9 %copy-start = (f32[6,384,1536]{2,1,0:T(8,128)}, f32[6,384,1536]{2,1,0:T(8,128)S(1)}, u32[]{:S(2)}) copy-start(f32[6,384,1536]{2,1,0:T(8,128)S(1)} %get-tuple-element.8) | copy-start | bytes 42467332
Sparse Core Ops, SparseCore 0:
  12.7 246.6 all-gather.6
  273.0 48.4 all-gather.8
  323.0 87.9 all-gather.10
  412.5 48.6 all-gather.12
  475.8 31.4 reduce-scatter.1
where the time goes:
time: 516 us
  waiting for transfers between devices  432 us (84%)
  matrix products  30.7 us (6%)
  local copies, waits for them, and re-layouts  18 us (3%)
  between operations  13.3 us (3%)
  blocking collectives  12.4 us (2%)
  other arithmetic  8.83 us (2%)
    all_gather x1, waiting for transfers between devices, local(): qkv = add_rows(normed, lax.all_gather(w_qkv, 'seq', axis=0, tiled=True))  244 us
    all_gather x1, waiting for transfers between devices, local(): lax.all_gather(w_out, 'seq', axis=2, tiled=True)  74.5 us
    all_gather x1, waiting for transfers between devices, local(): lax.all_gather(value_rows, 'seq', axis=0, tiled=True)  50.1 us
    all_gather x1, waiting for transfers between devices, local(): lax.all_gather(key_rows, 'seq', axis=0, tiled=True)  32.4 us
    reduce_scatter x1, waiting for transfers between devices, local(): lax.psum_scatter(head_terms.astype(jnp.bfloat16), ('tp', 'sub'), scatter_...  30.8 us
    unnamed x22, local copies, waits for them, and re-layouts  15.1 us
    dot_general x1, matrix products, local(): jnp.einsum('the,hec->tc', attended, lax.all_gather(w_out, 'seq', axis=2,...  14.5 us
    all_gather x1, blocking collectives, local(): lax.all_gather(key_valid, 'seq', axis=0, tiled=True)  12.4 us
  transfers between devices with their start and end apart: 5, of which 5 were waited for; matrix products, arithmetic and copies ran while one was open for 3% of the time, Pallas kernels for 0%

commit v1 on v0

--- a/solution.py
+++ b/solution.py
@@ -6,6 +6,17 @@
 
 HD = 128
 TILE = 384
+
+
+def ring_gather(x, axis, dim):
+    ways = lax.axis_size(axis)
+    pieces = [x]
+    for far in range(1, ways):
+        pieces.append(
+            lax.ppermute(pieces[far - 1], axis, [(d, (d - 1) % ways) for d in range(ways)])
+        )
+    line = jnp.concatenate(pieces, axis=dim)
+    return jnp.roll(line, lax.axis_index(axis) * x.shape[dim], axis=dim)
 
 
 def modulate(latents, mod_shift, mod_scale):
@@ -86,7 +97,7 @@
         tile_rows,
         start_state,
         (
-            lax.all_gather(key_rows, "seq", axis=0, tiled=True),
+            ring_gather(key_rows, "seq", 0),
             lax.all_gather(value_rows, "seq", axis=0, tiled=True),
             lax.all_gather(key_valid, "seq", axis=0, tiled=True),
         ),

time: 516 us -> 492 us (0.953)
  waiting for transfers between devices: 432 us -> 363 us
  blocking collectives: 12.4 us -> 48 us
  local copies, waits for them, and re-layouts: 18 us -> 24.9 us
    all_gather x1, waiting for transfers between devices: 74.5 us -> 0.02 us  [local(): lax.all_gather(w_out, 'seq', axis=2, tiled=True)]
    ppermute x0 -> x3, waiting for transfers between devices: none -> 59 us  [ring_gather(): lax.ppermute(pieces[far - 1], axis, [(d, (d - 1) % ways) for d in range(w...]
    all_gather x1, blocking collectives: 12.4 us -> 48 us  [local(): lax.all_gather(key_valid, 'seq', axis=0, tiled=True)]
    all_gather x1 -> x0, waiting for transfers between devices: 32.4 us -> none  [local(): lax.all_gather(key_rows, 'seq', axis=0, tiled=True)]
    all_gather x1, waiting for transfers between devices: 50.1 us -> 27.9 us  [local(): lax.all_gather(value_rows, 'seq', axis=0, tiled=True)]
    unnamed x22 -> x30, local copies, waits for them, and re-layouts: 15.1 us -> 21.2 us
  transfers between devices with their start and end apart: 5 -> 7, of which waited for: 5 -> 5; matrix products, arithmetic and copies ran while one was open for 3% -> 8% of each run, Pallas kernels for 0% -> 0%
where the time goes in v1:
time: 492 us; the launch traced here: 491 us
  waiting for transfers between devices  363 us (74%)
  blocking collectives  48 us (10%)
  matrix products  31.9 us (6%)
  local copies, waits for them, and re-layouts  24.9 us (5%)
  between operations  13.4 us (3%)
  other arithmetic  9.42 us (2%)
    all_gather x1, waiting for transfers between devices, local(): qkv = add_rows(normed, lax.all_gather(w_qkv, 'seq', axis=0, tiled=True))  245 us
    ppermute x3, waiting for transfers between devices, ring_gather(): lax.ppermute(pieces[far - 1], axis, [(d, (d - 1) % ways) for d in range(w...  59 us
    all_gather x1, blocking collectives, local(): lax.all_gather(key_valid, 'seq', axis=0, tiled=True)  48 us
    reduce_scatter x1, waiting for transfers between devices, local(): lax.psum_scatter(head_terms.astype(jnp.bfloat16), ('tp', 'sub'), scatter_...  30.8 us
    all_gather x1, waiting for transfers between devices, local(): lax.all_gather(value_rows, 'seq', axis=0, tiled=True)  27.9 us
    unnamed x30, local copies, waits for them, and re-layouts  21.2 us
    dot_general x1, matrix products, local(): jnp.einsum('the,hec->tc', attended, lax.all_gather(w_out, 'seq', axis=2,...  14.5 us
    unnamed x1, matrix products  10.7 us
  transfers between devices with their start and end apart: 7, of which 5 were waited for; matrix products, arithmetic and copies ran while one was open for 8% of the time, Pallas kernels for 0%

profile of v1, /device:TPU:0, one launch (start us, length us, event | category | flops | bytes accessed | tf_op | source)
XLA Modules:
  0.0 491.4 jit_solution(7662756561688399352)
XLA Ops:
  6.5 6.2 %copy.22 = bf16[768,3,6,128]{0,3,2,1:T(8,128)(2,1)} copy(bf16[768,3,6,128]{3,0,2,1:T(8,128)(2,1)} %param.12) | data formatting | bytes 7077888 | tf_op args[1]
  14.0 0.8 fusion.8
  14.8 244.8 %all-gather.6.cloned.1.call-done = bf16[3072,3,6,128]{0,3,2,1:T(8,128)(2,1)} async-done(((bf16[768,3,6,128]{0,3,2,1:T(8,128)(2,1)}), bf16[3072,3,6,128]{0,3,2,1:T(8,128)(2,1)}) %all-gather.6.cloned.1.call-update) | async-done | bytes 14155792 | tf_op jit(solution)/shard_map/all_gather | solution.py:81
  259.5 10.7 %fusion.13 = f32[384,2304]{0,1:S(1)} fusion(bf16[3072,2304]{0,1:T(8,128)(2,1)} %bitcast.46, bf16[384,3072]{1,0:T(8,128)(2,1)S(1)} %copy-done.1, f32[3072]{0:T(1024)S(1)} %copy-done.8, f32[3072]{0:T(1024)S(1)} %broadcast_add_fusion, f32[384]{0:T(512)S(1)} %add_rsqrt_fusion.2, f32[384]{0:T(512)S(1)} %broadcast_multiply_fusion), kind=kOutput, calls=%fused_computation.18 | convolution fusion | flops 5442895872 | bytes 20081664
  270.5 1.6 constant_dynamic-update-slice_fusion.7
  272.4 42.0 %collective-permute-done = bf16[384,6,128]{0,2,1:T(8,128)(2,1)S(1)} collective-permute-done((bf16[384,6,128]{0,2,1:T(8,128)(2,1)S(1)}, bf16[384,6,128]{0,2,1:T(8,128)(2,1)S(1)}, u32[]{:S(2)}, u32[]{:S(2)}) %collective-permute-start) | collective-permute-done | bytes 589856 | tf_op jit(solution)/shard_map/ppermute | solution.py:16
  314.3 48.0 %all-gather.1 = s32[4,1,384]{2,1,0:T(1,128)S(1)} all-gather(s32[1,1,384]{2,1,0:T(1,128)S(1)} %reshape.138), channel_id=1, replica_groups=mesh['rep'=2,'seq'=4,'tp'=2,'sub'=2] {'seq'}, dimensions={0}, use_global_device_ids=true | all-gather | bytes 7680 | tf_op jit(solution)/shard_map/all_gather | solution.py:102
  362.4 0.9 slice.28
  364.4 1.0 constant_dynamic-update-slice_fusion.6
  365.4 2.0 constant_dynamic-update-slice_fusion.5
  367.4 17.0 %collective-permute-done.2 = bf16[384,6,128]{0,2,1:T(8,128)(2,1)} collective-permute-done((bf16[384,6,128]{0,2,1:T(8,128)(2,1)}, bf16[384,6,128]{0,2,1:T(8,128)(2,1)}, u32[]{:S(2)}, u32[]{:S(2)}) %collective-permute-start.2) | collective-permute-done | bytes 589856 | tf_op jit(solution)/shard_map/ppermute | solution.py:16
  384.4 2.0 constant_dynamic-update-slice_fusion.4
  386.4 2.0 constant_dynamic-update-slice_fusion.3
  388.4 0.9 constant_dynamic-update-slice_fusion.2
  389.4 2.0 constant_dynamic-update-slice_fusion.1
  391.4 2.0 constant_dynamic-update-slice_fusion
  393.4 6.2 %fusion = (f32[6,384]{1,0:T(8,128)S(1)}, f32[6,384,1536]{2,1,0:T(8,128)S(1)}) fusion(pred[384,1536]{1,0:T(8,128)(4,1)S(1)} %fusion.12, bf16[3072,6,128]{0,2,1:T(8,128)(2,1)} %constant_dynamic-update-slice_fusion, s32[]{:T(128)S(6)} %select_n.36, f32[384,3,6,128]{0,3,2,1:T(8,128)} %bitcast.44, f32[128]{0:T(128)S(1)} %copy-done.6, ...), kind=kOutput, calls=%fused_computation.2 | convolution fusion | flops 917468928 | bytes 18303492 | tf_op jit(solution)/shard_map/qhe,khe->hqk/dot_general | solution.py:51
  399.6 5.0 %copy-done = f32[6,384,1536]{2,1,0:T(8,128)} copy-done((f32[6,384,1536]{2,1,0:T(8,128)}, f32[6,384,1536]{2,1,0:T(8,128)S(1)}, u32[]{:S(2)}) %copy-start) | copy-done | bytes 14155800
  404.7 4.2 fusion.1
  408.9 27.9 %all-gather.10.cloned.1.call-done = bf16[1536,1,6,128]{0,3,2,1:T(8,128)(2,1)} async-done(((bf16[384,1,6,128]{0,3,2,1:T(8,128)(2,1)}), bf16[1536,1,6,128]{0,3,2,1:T(8,128)(2,1)}) %all-gather.10.cloned.1.call-update) | async-done | bytes 2359312 | tf_op jit(solution)/shard_map/all_gather | solution.py:101
  436.8 14.5 %bitcast_convert_fusion = bf16[384,3072]{1,0:T(8,128)(2,1)} fusion(bf16[6,128,3072]{2,1,0:T(8,128)(2,1)} %all-gather.8.cloned.1.call-done, f32[6,384,1536]{2,1,0:T(8,128)} %copy-done, f32[6,384]{1,0:T(8,128)S(1)} %broadcast_maximum_fusion, pred[384,1536]{1,0:T(8,128)(4,1)S(1)} %fusion.12, bf16[1536,1,6,128]{0,3,2,1:T(8,128)(2,1)} %all-gather.10.cloned.1.call-done, ...), kind=kOutput, calls=%fused_computation.15 | convolution fusion | flops 2737373184 | bytes 24201216 | tf_op jit(solution)/shard_map/the,hec->tc/dot_general | solution.py:106
  451.3 0.8 dynamic_slice.11
  452.1 30.8 %reduce-scatter.2.cloned.1.call-done = bf16[384,768]{1,0:T(8,128)(2,1)} async-done(((bf16[384,3072]{1,0:T(8,128)(2,1)}), bf16[384,768]{1,0:T(8,128)(2,1)}) %reduce-scatter.2.cloned.1.call-update) | async-done | bytes 589840 | tf_op jit(solution)/shard_map/reduce_scatter | solution.py:112
  482.8 2.1 add_convert_fusion
  (50 shorter events, 2.8 us)
Async XLA Ops:
  6.5 7.0 %copy-start.1 = (bf16[384,3072]{1,0:T(8,128)(2,1)S(1)}, bf16[384,3072]{1,0:T(8,128)(2,1)}, u32[]{:S(2)}) copy-start(bf16[384,3072]{1,0:T(8,128)(2,1)} %param.11) | copy-start | bytes 7077892
  6.5 253.0 %all-gather.6.cloned.1.call-start = ((), (), s32[]{:S(2)}) async-start(), calls=%async_computation.1 | async-start | bytes 17694720 | tf_op jit(solution)/shard_map/all_gather | solution.py:81
  12.7 2.0 copy-start.4
  12.7 246.8 %copy-start.8 = (f32[3072]{0:T(1024)S(1)}, f32[3072]{0:T(1024)}, u32[]{:S(2)}) copy-start(f32[3072]{0:T(1024)} %param.16) | copy-start | bytes 36868
  12.8 396.2 %all-gather.8.cloned.1.call-start = ((), (), s32[]{:S(2)}) async-start(), calls=%async_computation.2 | async-start | bytes 5898240 | tf_op jit(solution)/shard_map/all_gather | solution.py:109
  13.5 423.3 %all-gather.10.cloned.1.call-start = ((), (), s32[]{:S(2)}) async-start(), calls=%async_computation.4 | async-start | bytes 2949120 | tf_op jit(solution)/shard_map/all_gather | solution.py:101
  259.5 11.0 %copy-start.7 = (f32[128]{0:T(128)S(1)}, f32[128]{0:T(128)}, u32[]{:S(2)}) copy-start(f32[128]{0:T(128)} %param.15) | copy-start | bytes 1540
  270.2 92.2 %copy-start.2 = (f32[384,2304]{0,1}, f32[384,2304]{0,1:S(1)}, u32[]{:S(2)}) copy-start(f32[384,2304]{0,1:S(1)} %fusion.13) | copy-start | bytes 10616836
  270.3 44.1 %copy-start.5 = (s32[384]{0:T(512)S(1)}, s32[384]{0:T(512)}, u32[]{:S(2)}) copy-start(s32[384]{0:T(512)} %param.21) | copy-start | bytes 4612
  270.3 92.1 %copy-start.9 = (s32[1,9]{1,0:T(1,128)S(1)}, s32[1,9]{1,0:T(1,128)}, u32[]{:S(2)}) copy-start(s32[1,9]{1,0:T(1,128)} %param.20) | copy-start | bytes 112
  270.3 93.1 %copy-start.10 = (s32[1,9]{1,0:T(1,128)S(1)}, s32[1,9]{1,0:T(1,128)}, u32[]{:S(2)}) copy-start(s32[1,9]{1,0:T(1,128)} %param.19) | copy-start | bytes 112
  272.1 42.2 %copy-start.3 = (bf16[384,6,128]{0,2,1:T(8,128)(2,1)}, bf16[384,6,128]{0,2,1:T(8,128)(2,1)S(1)}, u32[]{:S(2)}) copy-start(bf16[384,6,128]{0,2,1:T(8,128)(2,1)S(1)} %get-tuple-element.8) | copy-start | bytes 1769476
  272.1 42.2 %collective-permute-start = (bf16[384,6,128]{0,2,1:T(8,128)(2,1)S(1)}, bf16[384,6,128]{0,2,1:T(8,128)(2,1)S(1)}, u32[]{:S(2)}, u32[]{:S(2)}) collective-permute-start(bf16[384,6,128]{0,2,1:T(8,128)(2,1)S(1)} %get-tuple-element.8), channel_id=1, source_target_pairs={{0,12},{4,0},{8,4},{12,8},{1,13},{5,1},{9,5},{13,9},{2,14},{6,2},{... | collective-permute-start | bytes 1769480 | tf_op jit(solution)/shard_map/ppermute | solution.py:16
  314.3 49.2 %collective-permute-start.1 = (bf16[384,6,128]{0,2,1:T(8,128)(2,1)S(1)}, bf16[384,6,128]{0,2,1:T(8,128)(2,1)}, u32[]{:S(2)}, u32[]{:S(2)}) collective-permute-start(bf16[384,6,128]{0,2,1:T(8,128)(2,1)S(1)} %collective-permute-done), channel_id=1, source_target_pairs={{0,12},{4,0},{8,4},{12,8},{1,13},{5,1},{9,5},{13,9},{2,14},{6,2},{... | collective-permute-start | bytes 1769480 | tf_op jit(solution)/shard_map/ppermute | solution.py:16
  363.4 119.5 %reduce-scatter.2.cloned.1.call-start = ((), (), s32[]{:S(2)}) async-start(), calls=%async_computation.3 | async-start | bytes 2949120 | tf_op jit(solution)/shard_map/reduce_scatter | solution.py:112
  363.6 20.8 %collective-permute-start.2 = (bf16[384,6,128]{0,2,1:T(8,128)(2,1)}, bf16[384,6,128]{0,2,1:T(8,128)(2,1)}, u32[]{:S(2)}, u32[]{:S(2)}) collective-permute-start(bf16[384,6,128]{0,2,1:T(8,128)(2,1)} %collective-permute-done.1), channel_id=1, source_target_pairs={{0,12},{4,0},{8,4},{12,8},{1,13},{5,1},{9,5},{13,9},{2,14},{6,2},{... | collective-permute-start | bytes 1769480 | tf_op jit(solution)/shard_map/ppermute | solution.py:16
  364.4 29.0 %copy-start.6 = (f32[128]{0:T(128)S(1)}, f32[128]{0:T(128)}, u32[]{:S(2)}) copy-start(f32[128]{0:T(128)} %param.14) | copy-start | bytes 1540
  399.6 5.1 %copy-start = (f32[6,384,1536]{2,1,0:T(8,128)}, f32[6,384,1536]{2,1,0:T(8,128)S(1)}, u32[]{:S(2)}) copy-start(f32[6,384,1536]{2,1,0:T(8,128)S(1)} %get-tuple-element.10) | copy-start | bytes 42467332
Sparse Core Ops, SparseCore 0:
  12.9 246.6 all-gather.5
  261.1 117.4 all-gather.7
  380.2 56.4 all-gather.9
  451.4 31.4 reduce-scatter.1
